TPU v7x, 32 devices: a whole 2x2x4 slice. The times are simulated.
32 devices in a mesh: parts: 2 (over x), tile: 16 (over z, y, core).
Axes of the slice: x: 2, y: 2, z: 4, core: 2. Of those that a mesh axis runs over, the one named last changes fastest.
Arguments:
- sections: bfloat16 [4096, 2048], P(('parts', 'tile')), parts along dimension 0, may hold values from -10 to 10
- valid_mask: int32 [32, 16], P(('parts', 'tile')), parts along dimension 0, may hold values 0 or 1
- coarse_offsets: int32 [8, 2], P('parts'), parts along dimension 0, may hold values from -3 to 3
Outputs:
- aligned: bfloat16 [4096, 2048], P(('parts', 'tile')), parts along dimension 0
- node_shift: float32 [2, 32, 16], P(None, ('parts', 'tile')), parts along dimension 1
There are 2 independent parts, one for each index of `parts`. A program takes and returns all parts, laid end to end along the dimension named above; each array names one. Nothing has to cross between parts.
All inputs are finite; a program needn't handle non-finite values. No bound on the sum of `valid_mask` on one device may be relied on, other than what follows from the above.
Results may differ from a plain program's by a relative error of at most 0.002.
Values may be sent and summed in bfloat16 or wider, within the bound.
A program may use at most 64 MiB of HBM per device.

v0:
```python
import functools

import jax
import jax.numpy as jnp
import numpy as np
from jax import lax
from jax.experimental import pallas as pl
from jax.experimental.pallas import tpu as pltpu
from jax.sharding import PartitionSpec as P

SECTIONS = 4
PATCH = 128
HALF = 4
SWEEPS = 3
REACH = 3
WINDOW = 2 * HALF + 1
PADDED = 16
LANES = 128

sharpness = 12.0
anchor_weight = 2.0
MESH = pl.DeviceIdType.MESH
f32 = jnp.float32
bf16 = jnp.bfloat16


def split(value):
    high = value.astype(bf16)
    return high, (value - high.astype(f32)).astype(bf16)


def mm(a, b):
    return jnp.dot(a, b, preferred_element_type=f32)


def mm_nt(a, b):
    return lax.dot_general(a, b, (((1,), (1,)), ((), ())), preferred_element_type=f32)


def mm3(a, b, product=mm):
    return product(a[0], b[0]) + (product(a[0], b[1]) + product(a[1], b[0]))


def np_split(value):
    value = np.asarray(value, np.float32)
    high = np.asarray(value, bf16)
    low = np.asarray(value - high.astype(np.float32), bf16)
    return high, low


def constants():
    n = PATCH
    k = np.arange(n)
    angle = 2 * np.pi * ((k[:, None] * k[None, :]) % n) / n
    stacked = np.concatenate([np.cos(angle), np.sin(angle)], axis=0)
    dft_hi, dft_lo = np_split(stacked)
    dft_t_hi, dft_t_lo = np_split(stacked.T)
    u = np.arange(-HALF - REACH, -HALF - REACH + 24)
    window_angle = 2 * np.pi * ((u[:, None] * k[None, :]) % n) / n
    window = np.stack([np.cos(window_angle), np.sin(window_angle)]).astype(np.float32)
    gap = k[:, None] - k[None, :]
    half_angle = np.pi * gap / n
    warp = np.stack(
        [
            np.sin(half_angle),
            np.cos(half_angle),
            (1.0 - 2.0 * (gap % 2)) * np.ones((n, n)),
            gap % n,
        ]
    ).astype(np.float32)
    return dft_hi, dft_lo, dft_t_hi, dft_t_lo, window, warp


def shift_terms(d):
    whole = jnp.round(d)
    frac = d - whole
    odd = jnp.abs(whole - 2.0 * jnp.round(whole * 0.5))
    sine = jnp.sin(jnp.pi * frac)
    signed = jnp.where(odd > 0.5, -sine, sine) * (1.0 / PATCH)
    angle = d * (np.pi / PATCH)
    tangent = jnp.sin(angle) / jnp.cos(angle)
    small = frac * (np.pi / PATCH)
    tiny = jnp.abs(frac) < 1e-6
    peak = jnp.where(
        tiny, 1.0, sine * jnp.cos(small) / jnp.where(tiny, 1.0, PATCH * jnp.sin(small))
    )
    return tangent, signed, peak, whole


def interpolation(terms, tables, transposed):
    tangent, signed, peak, whole = terms
    sine, cosine, parity, gap = tables
    if transposed:
        bottom = cosine * tangent - sine
        top = cosine + sine * tangent
        centre = jnp.where(whole < 0, whole + PATCH, whole)
    else:
        bottom = cosine * tangent + sine
        top = cosine - sine * tangent
        centre = jnp.where(whole > 0, PATCH - whole, -whole)
    value = jnp.where(gap == centre, peak, (signed * parity) * (top / bottom))
    return split(value)


def warp_patch(patch, column, checker, tables):
    row_terms = [column[i : i + 1, :] for i in range(4)]
    col_terms = [column[i : i + 1, :] for i in range(4, 8)]
    right = interpolation(col_terms, tables, True)
    left = interpolation(row_terms, tables, False)
    inner = split(mm(patch, right[0]) + mm(patch, right[1]))
    corner = row_terms[1] * col_terms[1] * checker
    return mm3(left, inner) - corner * tables[2]


def total(value):
    return jnp.sum(jnp.sum(value, axis=0, keepdims=True), axis=1, keepdims=True)


def term_rows(d_rows, d_cols):
    both = jnp.concatenate([d_rows, d_cols], axis=0)
    tangent, signed, peak, whole = shift_terms(both)
    pieces = [t[i : i + 1] for i in range(2) for t in (tangent, signed, peak, whole)]
    return jnp.concatenate(pieces, axis=0)


def centred(patch):
    mean_level = total(patch) * (1.0 / (PATCH * PATCH))
    centre = patch - mean_level
    variance = total(centre * centre) * (1.0 / (PATCH * PATCH))
    return centre, jnp.sqrt(variance + 1e-05)


def patch_slices(width):
    return [slice(i * PATCH, (i + 1) * PATCH) for i in range(width // PATCH)]


def chain_kernel(
    tile_count,
    grid_cols,
    offsets,
    mask_ref,
    dft_hi,
    dft_lo,
    dft_t_hi,
    dft_t_lo,
    window,
    warp_tables,
    strip,
    out_ref,
    raw,
    mask_tile,
    mask_slots,
    flow_tile,
    flow_slots,
    spec_re,
    spec_im,
    local_sem,
    strip_send,
    strip_recv,
    mask_send,
    mask_recv,
    flow_send,
    flow_recv,
):
    per_section = tile_count // SECTIONS
    me = lax.axis_index("tile")
    lead = per_section // 2
    rotated = lax.rem(me + tile_count - lead, tile_count)
    group = rotated // per_section
    row = lax.rem(rotated, per_section)
    quarter = raw.shape[2]
    quarter_nodes = quarter // PATCH
    slices = patch_slices(quarter)

    barrier = pltpu.get_barrier_semaphore()
    for step in range(1, tile_count):
        peer = lax.rem(me + step, tile_count)
        pl.semaphore_signal(barrier, inc=1, device_id={"tile": peer}, device_id_type=MESH)

    own = pltpu.make_async_copy(
        strip.at[:, pl.ds(pl.multiple_of(group * quarter, LANES), quarter)],
        raw.at[group],
        local_sem,
    )
    own.start()
    shape = (2 * per_section, LANES)
    sub = lax.broadcasted_iota(jnp.int32, shape, 0)
    lane = lax.broadcasted_iota(jnp.int32, shape, 1)
    sub_row = lax.rem(sub, per_section)
    mask_tile[...] = jnp.zeros(shape, f32)
    mask_tile[0:1, 0:grid_cols] = mask_ref[...].astype(f32)
    mask_row = mask_tile[0:1, :]
    mask_tile[...] = jnp.where(sub_row == row, mask_row, 0.0)
    mask_slots[me] = mask_tile[...]

    pl.semaphore_wait(barrier, tile_count - 1)

    sends = []
    for step in range(1, SECTIONS):
        target_group = lax.rem(group + step, SECTIONS)
        target = lax.rem(me + step * per_section, tile_count)
        copy = pltpu.make_async_remote_copy(
            src_ref=strip.at[
                :, pl.ds(pl.multiple_of(target_group * quarter, LANES), quarter)
            ],
            dst_ref=raw.at[group],
            send_sem=strip_send.at[step],
            recv_sem=strip_recv.at[step],
            device_id={"tile": target},
            device_id_type=MESH,
        )
        copy.start()
        sends.append(copy)
    mask_copies = []
    for step in range(1, tile_count):
        peer = lax.rem(me + step, tile_count)
        copy = pltpu.make_async_remote_copy(
            src_ref=mask_tile,
            dst_ref=mask_slots.at[me],
            send_sem=mask_send.at[step],
            recv_sem=mask_recv.at[step],
            device_id={"tile": peer},
            device_id_type=MESH,
        )
        copy.start()
        mask_copies.append(copy)

    tables = [warp_tables[i] for i in range(4)]
    dft = (dft_hi[...], dft_lo[...])
    dft_t = (dft_t_hi[...], dft_t_lo[...])

    def spectra(centres):
        strip0 = jnp.concatenate(centres, axis=1)
        first = split(mm3(dft, split(strip0)))
        found = []
        for s in slices:
            both = mm3((first[0][:, s], first[1][:, s]), dft_t)
            real = both[:PATCH, :PATCH] - both[PATCH:, PATCH:]
            imag = -(both[:PATCH, PATCH:] + both[PATCH:, :PATCH])
            found.append((real, imag))
        return found

    def own_spectra(section):
        pieces = [centred(raw[section, :, s].astype(f32)) for s in slices]
        found = spectra([piece[0] for piece in pieces])
        for i, (real, imag) in enumerate(found):
            spec_re[i] = real
            spec_im[i] = imag
        return [piece[1] for piece in pieces]

    up_ok = (sub_row > 0).astype(f32)
    down_ok = (sub_row < per_section - 1).astype(f32)
    left_ok = jnp.logical_and(lane > 0, lane < grid_cols).astype(f32)
    right_ok = (lane < grid_cols - 1).astype(f32)
    count = up_ok + down_ok + left_ok + right_ok

    def relax(flow, mask):
        weight = anchor_weight * mask
        pull = weight * flow
        scale = 1.0 / (weight + count)
        d = flow * mask
        for _ in range(SWEEPS):
            near = (
                up_ok * pltpu.roll(d, 1, 0)
                + down_ok * pltpu.roll(d, 2 * per_section - 1, 0)
                + left_ok * pltpu.roll(d, 1, 1)
                + right_ok * pltpu.roll(d, LANES - 1, 1)
            )
            d = (pull + near) * scale
        return jnp.where(lane < grid_cols, d, 0.0)

    corr_row = lax.broadcasted_iota(jnp.int32, (PADDED, PADDED), 0)
    corr_col = lax.broadcasted_iota(jnp.int32, (PADDED, PADDED), 1)
    inside = jnp.logical_and(corr_row < WINDOW, corr_col < WINDOW)
    home = jnp.zeros(shape, f32)

    own.wait()
    for copy in sends:
        copy.wait()

    own_spread = own_spectra(1)
    d = None
    for section in range(1, SECTIONS):
        if section == 1:
            previous = [raw[0, :, s].astype(f32) for s in slices]
        else:
            pick_rows = jnp.sum(
                jnp.where(sub == row, d, 0.0), axis=0, keepdims=True
            )
            pick_cols = jnp.sum(
                jnp.where(sub == row + per_section, d, 0.0), axis=0, keepdims=True
            )
            terms = term_rows(pick_rows, pick_cols)
            term_lane = lax.broadcasted_iota(jnp.int32, terms.shape, 1)
            previous = []
            for i, s in enumerate(slices):
                wanted = term_lane == group * quarter_nodes + i
                column = jnp.sum(jnp.where(wanted, terms, 0.0), axis=1, keepdims=True)
                patch = raw[section - 1, :, s]
                checker = total(patch.astype(f32) * tables[2])
                moved = warp_patch(patch, column, checker, tables)
                previous.append(moved.astype(bf16).astype(f32))
        pieces = [centred(patch) for patch in previous]
        found = spectra([piece[0] for piece in pieces])
        row_offset = offsets[section, 0]
        col_offset = offsets[section, 1]
        row_cos = window[0, pl.ds(row_offset + REACH, PADDED), :]
        row_sin = window[1, pl.ds(row_offset + REACH, PADDED), :]
        col_cos = split(window[0, pl.ds(col_offset + REACH, PADDED), :])
        col_sin = split(window[1, pl.ds(col_offset + REACH, PADDED), :])
        row_table = split(jnp.concatenate([row_cos, row_sin], axis=0))
        row_shift = (corr_row - HALF + row_offset).astype(f32)
        col_shift = (corr_col - HALF + col_offset).astype(f32)
        half_re, half_im = [], []
        for i, (prev_re, prev_im) in enumerate(found):
            own_re, own_im = spec_re[i], spec_im[i]
            cross_re = own_re * prev_re + own_im * prev_im
            cross_im = own_im * prev_re - own_re * prev_im
            part_re = mm3(row_table, split(cross_re))
            part_im = mm3(row_table, split(cross_im))
            half_re.append(part_re[:PADDED] - part_im[PADDED:])
            half_im.append(part_im[:PADDED] + part_re[PADDED:])
        correlation = mm3(
            split(jnp.concatenate(half_re, axis=0)), col_cos, mm_nt
        ) - mm3(split(jnp.concatenate(half_im, axis=0)), col_sin, mm_nt)
        tile = jnp.zeros(shape, f32)
        for i in range(quarter_nodes):
            scale = sharpness / (float(PATCH) ** 4 * own_spread[i] * pieces[i][1])
            score = correlation[i * PADDED : (i + 1) * PADDED] * scale
            weights = jnp.where(inside, jnp.exp(score), 0.0)
            inverse = 1.0 / total(weights)
            flow_row = total(weights * row_shift) * inverse
            flow_col = total(weights * col_shift) * inverse
            here = lane == group * quarter_nodes + i
            tile = tile + jnp.where(
                jnp.logical_and(here, sub == row), flow_row, 0.0
            )
            tile = tile + jnp.where(
                jnp.logical_and(here, sub == row + per_section), flow_col, 0.0
            )
        index = section - 1
        flow_tile[index] = tile
        copies = []
        for step in range(1, tile_count):
            peer = lax.rem(me + step, tile_count)
            copy = pltpu.make_async_remote_copy(
                src_ref=flow_tile.at[index],
                dst_ref=flow_slots.at[index, step],
                send_sem=flow_send.at[index, step],
                recv_sem=flow_recv.at[index, step],
                device_id={"tile": peer},
                device_id_type=MESH,
            )
            copy.start()
            copies.append(copy)
        if section < SECTIONS - 1:
            own_spread = own_spectra(section + 1)
        if section == 1:
            for copy in mask_copies:
                copy.wait()
        mask = jnp.zeros(shape, f32)
        for r in range(per_section):
            mask = mask + mask_slots[(section * per_section + r + lead) % tile_count]
        for copy in copies:
            copy.wait()
        flow = tile
        for step in range(1, tile_count):
            flow = flow + flow_slots[index, step]
        d = relax(flow, mask)
        home = jnp.where(group == section, d, home)
    out_row = jnp.sum(jnp.where(sub == row, home, 0.0), axis=0, keepdims=True)
    out_col = jnp.sum(jnp.where(sub == row + per_section, home, 0.0), axis=0, keepdims=True)
    out_ref[...] = jnp.concatenate([out_row, out_col], axis=0)


def warp_kernel(shift_ref, strip, warp_tables, out_ref, node_ref):
    tables = [warp_tables[i] for i in range(4)]
    terms = term_rows(shift_ref[0:1, :], shift_ref[1:2, :])
    lane = lax.broadcasted_iota(jnp.int32, terms.shape, 1)
    nodes = node_ref.shape[2]
    node_ref[0] = shift_ref[0:1, 0:nodes]
    node_ref[1] = shift_ref[1:2, 0:nodes]
    for i, s in enumerate(patch_slices(strip.shape[1])):
        column = jnp.sum(jnp.where(lane == i, terms, 0.0), axis=1, keepdims=True)
        patch = strip[:, s]
        checker = total(patch.astype(f32) * tables[2])
        out_ref[:, s] = warp_patch(patch, column, checker, tables).astype(bf16)


def shards(tile_count, sections, valid_mask, coarse_offsets):
    dft_hi, dft_lo, dft_t_hi, dft_t_lo, window, warp = constants()
    per_section = tile_count // SECTIONS
    grid_cols = valid_mask.shape[1]
    quarter = sections.shape[1] // SECTIONS
    nodes = quarter // PATCH
    steps = SECTIONS - 1
    tile_shape = (2 * per_section, LANES)
    vmem = pl.BlockSpec(memory_space=pltpu.VMEM)
    shift = pl.pallas_call(
        functools.partial(chain_kernel, tile_count, grid_cols),
        out_shape=jax.ShapeDtypeStruct((2, LANES), f32),
        in_specs=[pl.BlockSpec(memory_space=pltpu.SMEM)]
        + [vmem] * 7
        + [pl.BlockSpec(memory_space=pl.ANY)],
        out_specs=vmem,
        scratch_shapes=[
            pltpu.VMEM((SECTIONS, PATCH, quarter), bf16),
            pltpu.VMEM(tile_shape, f32),
            pltpu.VMEM((tile_count,) + tile_shape, f32),
            pltpu.VMEM((steps,) + tile_shape, f32),
            pltpu.VMEM((steps, tile_count) + tile_shape, f32),
            pltpu.VMEM((nodes, PATCH, PATCH), f32),
            pltpu.VMEM((nodes, PATCH, PATCH), f32),
            pltpu.SemaphoreType.DMA,
            pltpu.SemaphoreType.DMA((SECTIONS,)),
            pltpu.SemaphoreType.DMA((SECTIONS,)),
            pltpu.SemaphoreType.DMA((tile_count,)),
            pltpu.SemaphoreType.DMA((tile_count,)),
            pltpu.SemaphoreType.DMA((steps, tile_count)),
            pltpu.SemaphoreType.DMA((steps, tile_count)),
        ],
        compiler_params=pltpu.CompilerParams(
            collective_id=0, has_side_effects=True, vmem_limit_bytes=48 * 1024 * 1024
        ),
        name="chain",
    )(coarse_offsets, valid_mask, dft_hi, dft_lo, dft_t_hi, dft_t_lo, window, warp, sections)
    return pl.pallas_call(
        warp_kernel,
        out_shape=(
            jax.ShapeDtypeStruct(sections.shape, bf16),
            jax.ShapeDtypeStruct((2, 1, grid_cols), f32),
        ),
        in_specs=[vmem, vmem, vmem],
        out_specs=(vmem, vmem),
        name="warp",
    )(shift, sections, warp)


def solution(mesh):
    placed = (P(("parts", "tile"), None), P(("parts", "tile"), None), P("parts", None))
    return jax.shard_map(
        functools.partial(shards, mesh.shape["tile"]),
        mesh=mesh,
        in_specs=placed,
        out_specs=(P(("parts", "tile"), None), P(None, ("parts", "tile"), None)),
        check_vma=False,
    )
```

profile of v0, /device:TPU:0, one launch (start us, length us, event | category | flops | bytes accessed | tf_op | source)
XLA Modules:
  0.0 53.5 jit_solution(10220641465557390795)
XLA Ops:
  0.6 0.0 copy-start.8
  0.6 0.8 %copy.11.offsets = s32[4,2]{1,0:T(4,128)S(1)} copy(s32[4,2]{0,1:T(2,128)} %param.11) | data formatting | bytes 64 | tf_op args[2]
  1.4 0.0 copy-done.8
  1.4 0.0 copy-start
  1.4 1.0 %copy-done = bf16[128,2048]{1,0:T(8,128)(2,1)S(1)} copy-done((bf16[128,2048]{1,0:T(8,128)(2,1)S(1)}, bf16[128,2048]{1,0:T(8,128)(2,1)}, u32[]{:S(2)}) %copy-start) | copy-done | bytes 524312
  2.5 0.0 copy-start.1
  2.5 0.9 %copy-done.1 = f32[4,128,128]{2,1,0:T(8,128)S(1)} copy-done((f32[4,128,128]{2,1,0:T(8,128)S(1)}, f32[4,128,128]{2,1,0:T(8,128)}, u32[]{:S(2)}) %copy-start.1) | copy-done | bytes 262168
  3.4 0.0 copy-start.2
  3.4 0.8 %copy-done.2 = bf16[128,256]{1,0:T(8,128)(2,1)S(1)} copy-done((bf16[128,256]{1,0:T(8,128)(2,1)S(1)}, bf16[128,256]{1,0:T(8,128)(2,1)}, u32[]{:S(2)}) %copy-start.2) | copy-done | bytes 65560
  4.2 0.0 copy-start.3
  4.2 0.8 %copy-done.3 = bf16[128,256]{1,0:T(8,128)(2,1)S(1)} copy-done((bf16[128,256]{1,0:T(8,128)(2,1)S(1)}, bf16[128,256]{1,0:T(8,128)(2,1)}, u32[]{:S(2)}) %copy-start.3) | copy-done | bytes 65560
  5.1 0.0 copy-start.4
  5.1 0.8 %copy-done.4 = bf16[256,128]{1,0:T(8,128)(2,1)S(1)} copy-done((bf16[256,128]{1,0:T(8,128)(2,1)S(1)}, bf16[256,128]{1,0:T(8,128)(2,1)}, u32[]{:S(2)}) %copy-start.4) | copy-done | bytes 65560
  5.9 0.0 copy-start.5
  5.9 0.8 %copy-done.5 = bf16[256,128]{1,0:T(8,128)(2,1)S(1)} copy-done((bf16[256,128]{1,0:T(8,128)(2,1)S(1)}, bf16[256,128]{1,0:T(8,128)(2,1)}, u32[]{:S(2)}) %copy-start.5) | copy-done | bytes 65560
  6.8 0.0 copy-start.6
  6.8 0.7 %copy-done.6 = f32[2,24,128]{2,1,0:T(8,128)S(1)} copy-done((f32[2,24,128]{2,1,0:T(8,128)S(1)}, f32[2,24,128]{2,1,0:T(8,128)}, u32[]{:S(2)}) %copy-start.6) | copy-done | bytes 24600
  7.5 41.3 %chain.1.shift_ref = f32[2,128]{1,0:T(2,128)S(1)} custom-call(s32[4,2]{1,0:T(4,128)S(1)} %copy.11.offsets, s32[1,16]{1,0:T(1,128)S(1)} %copy-done.8, bf16[256,128]{1,0:T(8,128)(2,1)S(1)} %copy-done.5, bf16[256,128]{1,0:T(8,128)(2,1)S(1)} %copy-done.4, bf16[128,256]{1,0:T(8,128)(2,1)S(1)} %copy-done.3, bf16[128,256]{1,0:T(8,128)(2,1)S(1)} %copy-done.2, ...), custom_call_target="tpu_custom_call" | custom-call | tf_op jit(solution)/shard_map/chain/pallas_call | solution.py:399
  48.8 0.0 copy-start.7
  48.8 0.6 %copy-done.7 = f32[2,128]{1,0:T(2,128)} copy-done((f32[2,128]{1,0:T(2,128)}, f32[2,128]{1,0:T(2,128)S(1)}, u32[]{:S(2)}) %copy-start.7) | copy-done | bytes 1048
  49.3 4.2 %warp.1 = (bf16[128,2048]{1,0:T(8,128)(2,1)}, f32[2,1,16]{2,1,0:T(1,128)}) custom-call(f32[2,128]{1,0:T(2,128)} %copy-done.7, bf16[128,2048]{1,0:T(8,128)(2,1)} %strip.3, f32[4,128,128]{2,1,0:T(8,128)} %constant.17.clone.warp_tables), custom_call_target="tpu_custom_call" | custom-call | tf_op jit(solution)/shard_map/warp/pallas_call | solution.py:427
Async XLA Ops:
  0.6 0.8 %copy-start.8 = (s32[1,16]{1,0:T(1,128)S(1)}, s32[1,16]{1,0:T(1,128)}, u32[]{:S(2)}) copy-start(s32[1,16]{1,0:T(1,128)} %mask_ref.1) | copy-start | bytes 196
  1.4 1.0 %copy-start = (bf16[128,2048]{1,0:T(8,128)(2,1)S(1)}, bf16[128,2048]{1,0:T(8,128)(2,1)}, u32[]{:S(2)}) copy-start(bf16[128,2048]{1,0:T(8,128)(2,1)} %strip.3) | copy-start | bytes 1572868
  2.5 0.9 %copy-start.1 = (f32[4,128,128]{2,1,0:T(8,128)S(1)}, f32[4,128,128]{2,1,0:T(8,128)}, u32[]{:S(2)}) copy-start(f32[4,128,128]{2,1,0:T(8,128)} %constant.17.clone.warp_tables) | copy-start | bytes 786436
  3.4 0.8 %copy-start.2 = (bf16[128,256]{1,0:T(8,128)(2,1)S(1)}, bf16[128,256]{1,0:T(8,128)(2,1)}, u32[]{:S(2)}) copy-start(bf16[128,256]{1,0:T(8,128)(2,1)} %constant.15.clone.dft_t_lo) | copy-start | bytes 196612
  4.2 0.8 %copy-start.3 = (bf16[128,256]{1,0:T(8,128)(2,1)S(1)}, bf16[128,256]{1,0:T(8,128)(2,1)}, u32[]{:S(2)}) copy-start(bf16[128,256]{1,0:T(8,128)(2,1)} %constant.14.clone.dft_t_hi) | copy-start | bytes 196612
  5.1 0.8 %copy-start.4 = (bf16[256,128]{1,0:T(8,128)(2,1)S(1)}, bf16[256,128]{1,0:T(8,128)(2,1)}, u32[]{:S(2)}) copy-start(bf16[256,128]{1,0:T(8,128)(2,1)} %constant.13.clone.dft_lo) | copy-start | bytes 196612
  5.9 0.8 %copy-start.5 = (bf16[256,128]{1,0:T(8,128)(2,1)S(1)}, bf16[256,128]{1,0:T(8,128)(2,1)}, u32[]{:S(2)}) copy-start(bf16[256,128]{1,0:T(8,128)(2,1)} %constant.12.clone.dft_hi) | copy-start | bytes 196612
  6.8 0.7 %copy-start.6 = (f32[2,24,128]{2,1,0:T(8,128)S(1)}, f32[2,24,128]{2,1,0:T(8,128)}, u32[]{:S(2)}) copy-start(f32[2,24,128]{2,1,0:T(8,128)} %constant.16.clone.window) | copy-start | bytes 73732
  48.8 0.6 %copy-start.7 = (f32[2,128]{1,0:T(2,128)}, f32[2,128]{1,0:T(2,128)S(1)}, u32[]{:S(2)}) copy-start(f32[2,128]{1,0:T(2,128)S(1)} %chain.1.shift_ref) | copy-start | bytes 3076
where the time goes:
time: 54 us; the launch traced here: 53.5 us
  Pallas kernels  45.4 us (84%)
  local copies, waits for them, and re-layouts  7.43 us (14%)
  between operations  0.66 us (1%)
    pallas_call x1, Pallas kernels, shards(): pl.pallas_call(functools.partial(chain_kernel, tile_count, grid_cols), ou...  41.3 us
    unnamed x19, local copies, waits for them, and re-layouts  7.43 us
    pallas_call x1, Pallas kernels, shards(): pl.pallas_call(warp_kernel, out_shape=(jax.ShapeDtypeStruct(sections.shap...  4.17 us

commit v1 on v0

--- a/solution.py
+++ b/solution.py
@@ -16,6 +16,9 @@
 WINDOW = 2 * HALF + 1
 PADDED = 16
 LANES = 128
+CONSTANTS = 6
+HALVES = 2
+PIECES = 4
 
 sharpness = 12.0
 anchor_weight = 2.0
@@ -137,52 +140,67 @@
 def chain_kernel(
     tile_count,
     grid_cols,
+    offsets_in,
+    mask_in,
+    *rest,
+):
+    constant_in = rest[:CONSTANTS]
+    constant_ref = rest[CONSTANTS + 2 : 2 * CONSTANTS + 2]
+    (dft_hi, dft_lo, dft_t_hi, dft_t_lo, window, warp_tables) = constant_ref
+    strip, out_ref = rest[CONSTANTS : CONSTANTS + 2]
+    (
     offsets,
     mask_ref,
-    dft_hi,
-    dft_lo,
-    dft_t_hi,
-    dft_t_lo,
-    window,
-    warp_tables,
-    strip,
-    out_ref,
+    load_sem,
     raw,
     mask_tile,
     mask_slots,
     flow_tile,
     flow_slots,
+    flow_sum,
     spec_re,
     spec_im,
-    local_sem,
     strip_send,
     strip_recv,
     mask_send,
     mask_recv,
     flow_send,
     flow_recv,
-):
+    ) = rest[2 * CONSTANTS + 2 :]
     per_section = tile_count // SECTIONS
     me = lax.axis_index("tile")
     lead = per_section // 2
     rotated = lax.rem(me + tile_count - lead, tile_count)
     group = rotated // per_section
     row = lax.rem(rotated, per_section)
-    quarter = raw.shape[2]
+    chain = me // per_section
+    quarter = raw.shape[3] * HALVES
+    part = raw.shape[3]
     quarter_nodes = quarter // PATCH
-    slices = patch_slices(quarter)
+    part_nodes = part // PATCH
+    reach = -(-SWEEPS // quarter_nodes)
 
     barrier = pltpu.get_barrier_semaphore()
     for step in range(1, tile_count):
         peer = lax.rem(me + step, tile_count)
         pl.semaphore_signal(barrier, inc=1, device_id={"tile": peer}, device_id_type=MESH)
 
-    own = pltpu.make_async_copy(
-        strip.at[:, pl.ds(pl.multiple_of(group * quarter, LANES), quarter)],
-        raw.at[group],
-        local_sem,
-    )
-    own.start()
+    loads = [
+        pltpu.make_async_copy(source, target, load_sem.at[i])
+        for i, (source, target) in enumerate(
+            zip((mask_in, offsets_in) + constant_in, (mask_ref, offsets) + constant_ref)
+        )
+    ]
+    for copy in loads:
+        copy.start()
+    def columns(owner, half):
+        return strip.at[:, pl.ds(pl.multiple_of(owner * quarter + half * part, LANES), part)]
+
+    for half in range(HALVES):
+        pltpu.make_async_copy(
+            columns(chain, half), raw.at[group, half], strip_recv.at[group, half]
+        ).start()
+    loads[0].wait()
     shape = (2 * per_section, LANES)
     sub = lax.broadcasted_iota(jnp.int32, shape, 0)
     lane = lax.broadcasted_iota(jnp.int32, shape, 1)
@@ -195,22 +213,6 @@
 
     pl.semaphore_wait(barrier, tile_count - 1)
 
-    sends = []
-    for step in range(1, SECTIONS):
-        target_group = lax.rem(group + step, SECTIONS)
-        target = lax.rem(me + step * per_section, tile_count)
-        copy = pltpu.make_async_remote_copy(
-            src_ref=strip.at[
-                :, pl.ds(pl.multiple_of(target_group * quarter, LANES), quarter)
-            ],
-            dst_ref=raw.at[group],
-            send_sem=strip_send.at[step],
-            recv_sem=strip_recv.at[step],
-            device_id={"tile": target},
-            device_id_type=MESH,
-        )
-        copy.start()
-        sends.append(copy)
     mask_copies = []
     for step in range(1, tile_count):
         peer = lax.rem(me + step, tile_count)
@@ -225,6 +227,21 @@
         copy.start()
         mask_copies.append(copy)
 
+    sends = []
+    for half in range(HALVES):
+        for step in range(1, SECTIONS):
+            copy = pltpu.make_async_remote_copy(
+                src_ref=columns(lax.rem(chain + step, SECTIONS), half),
+                dst_ref=raw.at[group, half],
+                send_sem=strip_send.at[step, half],
+                recv_sem=strip_recv.at[group, half],
+                device_id={"tile": lax.rem(me + step * per_section, tile_count)},
+                device_id_type=MESH,
+            )
+            copy.start()
+            sends.append(copy)
+    for copy in loads[1:]:
+        copy.wait()
     tables = [warp_tables[i] for i in range(4)]
     dft = (dft_hi[...], dft_lo[...])
     dft_t = (dft_t_hi[...], dft_t_lo[...])
@@ -233,20 +250,27 @@
         strip0 = jnp.concatenate(centres, axis=1)
         first = split(mm3(dft, split(strip0)))
         found = []
-        for s in slices:
+        for s in patch_slices(strip0.shape[1]):
             both = mm3((first[0][:, s], first[1][:, s]), dft_t)
             real = both[:PATCH, :PATCH] - both[PATCH:, PATCH:]
             imag = -(both[:PATCH, PATCH:] + both[PATCH:, :PATCH])
             found.append((real, imag))
         return found
 
-    def own_spectra(section):
-        pieces = [centred(raw[section, :, s].astype(f32)) for s in slices]
+    def patch_of(section, i):
+        start = (i % part_nodes) * PATCH
+        return raw[section, i // part_nodes, :, start : start + PATCH]
+
+    def own_spectra(section, nodes):
+        pieces = [centred(patch_of(section, i).astype(f32)) for i in nodes]
         found = spectra([piece[0] for piece in pieces])
-        for i, (real, imag) in enumerate(found):
+        for i, (real, imag) in zip(nodes, found):
             spec_re[i] = real
             spec_im[i] = imag
         return [piece[1] for piece in pieces]
+
+    def checkers(section):
+        return [total(patch_of(section, i).astype(f32) * tables[2]) for i in range(quarter_nodes)]
 
     up_ok = (sub_row > 0).astype(f32)
     down_ok = (sub_row < per_section - 1).astype(f32)
@@ -272,38 +296,17 @@
     corr_row = lax.broadcasted_iota(jnp.int32, (PADDED, PADDED), 0)
     corr_col = lax.broadcasted_iota(jnp.int32, (PADDED, PADDED), 1)
     inside = jnp.logical_and(corr_row < WINDOW, corr_col < WINDOW)
-    home = jnp.zeros(shape, f32)
-
-    own.wait()
-    for copy in sends:
-        copy.wait()
-
-    own_spread = own_spectra(1)
-    d = None
-    for section in range(1, SECTIONS):
-        if section == 1:
-            previous = [raw[0, :, s].astype(f32) for s in slices]
-        else:
-            pick_rows = jnp.sum(
-                jnp.where(sub == row, d, 0.0), axis=0, keepdims=True
-            )
-            pick_cols = jnp.sum(
-                jnp.where(sub == row + per_section, d, 0.0), axis=0, keepdims=True
-            )
-            terms = term_rows(pick_rows, pick_cols)
-            term_lane = lax.broadcasted_iota(jnp.int32, terms.shape, 1)
-            previous = []
-            for i, s in enumerate(slices):
-                wanted = term_lane == group * quarter_nodes + i
-                column = jnp.sum(jnp.where(wanted, terms, 0.0), axis=1, keepdims=True)
-                patch = raw[section - 1, :, s]
-                checker = total(patch.astype(f32) * tables[2])
-                moved = warp_patch(patch, column, checker, tables)
-                previous.append(moved.astype(bf16).astype(f32))
+
+    def arrived(section, half):
+        pltpu.make_async_copy(
+            raw.at[section, half], raw.at[section, half], strip_recv.at[section, half]
+        ).wait()
+
+    def flows(section, previous, own_spread, nodes):
         pieces = [centred(patch) for patch in previous]
         found = spectra([piece[0] for piece in pieces])
-        row_offset = offsets[section, 0]
-        col_offset = offsets[section, 1]
+        row_offset = offsets[0, section]
+        col_offset = offsets[1, section]
         row_cos = window[0, pl.ds(row_offset + REACH, PADDED), :]
         row_sin = window[1, pl.ds(row_offset + REACH, PADDED), :]
         col_cos = split(window[0, pl.ds(col_offset + REACH, PADDED), :])
@@ -312,7 +315,7 @@
         row_shift = (corr_row - HALF + row_offset).astype(f32)
         col_shift = (corr_col - HALF + col_offset).astype(f32)
         half_re, half_im = [], []
-        for i, (prev_re, prev_im) in enumerate(found):
+        for i, (prev_re, prev_im) in zip(nodes, found):
             own_re, own_im = spec_re[i], spec_im[i]
             cross_re = own_re * prev_re + own_im * prev_im
             cross_im = own_im * prev_re - own_re * prev_im
@@ -324,71 +327,156 @@
             split(jnp.concatenate(half_re, axis=0)), col_cos, mm_nt
         ) - mm3(split(jnp.concatenate(half_im, axis=0)), col_sin, mm_nt)
         tile = jnp.zeros(shape, f32)
-        for i in range(quarter_nodes):
-            scale = sharpness / (float(PATCH) ** 4 * own_spread[i] * pieces[i][1])
-            score = correlation[i * PADDED : (i + 1) * PADDED] * scale
+        for k, i in enumerate(nodes):
+            scale = sharpness / (float(PATCH) ** 4 * own_spread[k] * pieces[k][1])
+            score = correlation[k * PADDED : (k + 1) * PADDED] * scale
             weights = jnp.where(inside, jnp.exp(score), 0.0)
             inverse = 1.0 / total(weights)
             flow_row = total(weights * row_shift) * inverse
             flow_col = total(weights * col_shift) * inverse
-            here = lane == group * quarter_nodes + i
-            tile = tile + jnp.where(
-                jnp.logical_and(here, sub == row), flow_row, 0.0
+            here = lane == chain * quarter_nodes + i
+            tile = jnp.where(jnp.logical_and(here, sub == row), flow_row, tile)
+            tile = jnp.where(
+                jnp.logical_and(here, sub == row + per_section), flow_col, tile
             )
-            tile = tile + jnp.where(
-                jnp.logical_and(here, sub == row + per_section), flow_col, 0.0
+        return tile
+
+    def receive(index, away):
+        def take(other):
+            pltpu.make_async_copy(
+                flow_slots.at[index, other], flow_slots.at[index, other], flow_recv.at[index, other]
+            ).wait()
+            return flow_slots[index, other]
+
+        base = (chain + away) * per_section
+        if away == 0:
+            mine = lax.rem(me, per_section)
+            found = flow_sum[index]
+            for j in range(1, per_section):
+                found = found + take(base + lax.rem(mine + j, per_section))
+            flow_sum[index] = found
+        else:
+
+            @pl.when(jnp.logical_and(chain + away >= 0, chain + away < SECTIONS))
+            def _():
+                found = flow_sum[index]
+                for j in range(per_section):
+                    found = found + take(base + j)
+                flow_sum[index] = found
+
+    everyone = list(range(quarter_nodes))
+    d = None
+    for section in range(1, SECTIONS):
+        index = section - 1
+        if section == 1:
+            tile = jnp.zeros(shape, f32)
+            for half in range(HALVES):
+                nodes = everyone[half * part_nodes : (half + 1) * part_nodes]
+                arrived(1, half)
+                arrived(0, half)
+                spread = own_spectra(1, nodes)
+                previous = [patch_of(0, i).astype(f32) for i in nodes]
+                tile = tile + flows(1, previous, spread, nodes)
+        else:
+            pick_rows = jnp.sum(
+                jnp.where(sub == row, d, 0.0), axis=0, keepdims=True
             )
-        index = section - 1
+            pick_cols = jnp.sum(
+                jnp.where(sub == row + per_section, d, 0.0), axis=0, keepdims=True
+            )
+            terms = term_rows(pick_rows, pick_cols)
+            term_lane = lax.broadcasted_iota(jnp.int32, terms.shape, 1)
+            previous = []
+            for i in everyone:
+                wanted = term_lane == chain * quarter_nodes + i
+                column = jnp.sum(jnp.where(wanted, terms, 0.0), axis=1, keepdims=True)
+                moved = warp_patch(patch_of(index, i), column, corners[i], tables)
+                previous.append(moved.astype(bf16).astype(f32))
+            tile = flows(section, previous, spread, everyone)
         flow_tile[index] = tile
+        flow_sum[index] = tile
         copies = []
         for step in range(1, tile_count):
             peer = lax.rem(me + step, tile_count)
             copy = pltpu.make_async_remote_copy(
                 src_ref=flow_tile.at[index],
-                dst_ref=flow_slots.at[index, step],
+                dst_ref=flow_slots.at[index, me],
                 send_sem=flow_send.at[index, step],
-                recv_sem=flow_recv.at[index, step],
+                recv_sem=flow_recv.at[index, me],
                 device_id={"tile": peer},
                 device_id_type=MESH,
             )
             copy.start()
             copies.append(copy)
-        if section < SECTIONS - 1:
-            own_spread = own_spectra(section + 1)
         if section == 1:
             for copy in mask_copies:
                 copy.wait()
-        mask = jnp.zeros(shape, f32)
-        for r in range(per_section):
-            mask = mask + mask_slots[(section * per_section + r + lead) % tile_count]
-        for copy in copies:
-            copy.wait()
-        flow = tile
-        for step in range(1, tile_count):
-            flow = flow + flow_slots[index, step]
-        d = relax(flow, mask)
-        home = jnp.where(group == section, d, home)
+        if section < SECTIONS - 1:
+            for half in range(HALVES):
+                arrived(section + 1, half)
+            spread = own_spectra(section + 1, everyone)
+            corners = checkers(section)
+            mask = jnp.zeros(shape, f32)
+            for r in range(per_section):
+                mask = mask + mask_slots[(section * per_section + r + lead) % tile_count]
+            for away in range(-reach, reach + 1):
+                receive(index, away)
+            d = relax(flow_sum[index], mask)
+        sends += copies
+    mask = jnp.zeros(shape, f32)
+    for r in range(per_section):
+        mask = mask + mask_slots[
+            lax.rem(group * per_section + r + lead, tile_count)
+        ]
+    for copy in sends:
+        copy.wait_send()
+    for index in range(SECTIONS - 1):
+        for away in range(1 - SECTIONS, SECTIONS):
+            if abs(away) > reach or index == SECTIONS - 2:
+                receive(index, away)
+    flow = jnp.zeros(shape, f32)
+    for index in range(SECTIONS - 1):
+        flow = jnp.where(group == index + 1, flow_sum[index], flow)
+    home = jnp.where(group == 0, 0.0, relax(flow, mask))
     out_row = jnp.sum(jnp.where(sub == row, home, 0.0), axis=0, keepdims=True)
     out_col = jnp.sum(jnp.where(sub == row + per_section, home, 0.0), axis=0, keepdims=True)
     out_ref[...] = jnp.concatenate([out_row, out_col], axis=0)
 
 
-def warp_kernel(shift_ref, strip, warp_tables, out_ref, node_ref):
-    tables = [warp_tables[i] for i in range(4)]
+def warp_kernel(shift_ref, strip_in, tables_in, out, node_ref, strip, warp_tables, result, sems):
+    pieces = strip.shape[0]
+    width = strip.shape[2]
+    table_load = pltpu.make_async_copy(tables_in, warp_tables, sems.at[2 * pieces])
+    table_load.start()
+    loads, stores = [], []
+    for k in range(pieces):
+        where = pl.ds(k * width, width)
+        loads.append(pltpu.make_async_copy(strip_in.at[:, where], strip.at[k], sems.at[k]))
+        stores.append(
+            pltpu.make_async_copy(result.at[k], out.at[:, where], sems.at[pieces + k])
+        )
+        loads[k].start()
     terms = term_rows(shift_ref[0:1, :], shift_ref[1:2, :])
     lane = lax.broadcasted_iota(jnp.int32, terms.shape, 1)
     nodes = node_ref.shape[2]
     node_ref[0] = shift_ref[0:1, 0:nodes]
     node_ref[1] = shift_ref[1:2, 0:nodes]
-    for i, s in enumerate(patch_slices(strip.shape[1])):
-        column = jnp.sum(jnp.where(lane == i, terms, 0.0), axis=1, keepdims=True)
-        patch = strip[:, s]
-        checker = total(patch.astype(f32) * tables[2])
-        out_ref[:, s] = warp_patch(patch, column, checker, tables).astype(bf16)
+    table_load.wait()
+    tables = [warp_tables[i] for i in range(4)]
+    for k in range(pieces):
+        loads[k].wait()
+        for j, s in enumerate(patch_slices(width)):
+            i = k * (width // PATCH) + j
+            column = jnp.sum(jnp.where(lane == i, terms, 0.0), axis=1, keepdims=True)
+            patch = strip[k, :, s]
+            checker = total(patch.astype(f32) * tables[2])
+            result[k, :, s] = warp_patch(patch, column, checker, tables).astype(bf16)
+        stores[k].start()
+    for copy in stores:
+        copy.wait()
 
 
 def shards(tile_count, sections, valid_mask, coarse_offsets):
-    dft_hi, dft_lo, dft_t_hi, dft_t_lo, window, warp = constants()
     per_section = tile_count // SECTIONS
     grid_cols = valid_mask.shape[1]
     quarter = sections.shape[1] // SECTIONS
@@ -396,44 +484,54 @@
     steps = SECTIONS - 1
     tile_shape = (2 * per_section, LANES)
     vmem = pl.BlockSpec(memory_space=pltpu.VMEM)
+    tables = constants()
+    hbm = pl.BlockSpec(memory_space=pltpu.HBM)
     shift = pl.pallas_call(
         functools.partial(chain_kernel, tile_count, grid_cols),
         out_shape=jax.ShapeDtypeStruct((2, LANES), f32),
-        in_specs=[pl.BlockSpec(memory_space=pltpu.SMEM)]
-        + [vmem] * 7
-        + [pl.BlockSpec(memory_space=pl.ANY)],
+        in_specs=[hbm] * (CONSTANTS + 3),
         out_specs=vmem,
-        scratch_shapes=[
-            pltpu.VMEM((SECTIONS, PATCH, quarter), bf16),
+        scratch_shapes=[pltpu.VMEM(table.shape, table.dtype) for table in tables]
+        + [
+            pltpu.SMEM(coarse_offsets.shape[::-1], jnp.int32),
+            pltpu.VMEM(valid_mask.shape, jnp.int32),
+            pltpu.SemaphoreType.DMA((CONSTANTS + 2,)),
+            pltpu.VMEM((SECTIONS, HALVES, PATCH, quarter // HALVES), bf16),
             pltpu.VMEM(tile_shape, f32),
             pltpu.VMEM((tile_count,) + tile_shape, f32),
             pltpu.VMEM((steps,) + tile_shape, f32),
             pltpu.VMEM((steps, tile_count) + tile_shape, f32),
+            pltpu.VMEM((steps,) + tile_shape, f32),
             pltpu.VMEM((nodes, PATCH, PATCH), f32),
             pltpu.VMEM((nodes, PATCH, PATCH), f32),
-            pltpu.SemaphoreType.DMA,
-            pltpu.SemaphoreType.DMA((SECTIONS,)),
-            pltpu.SemaphoreType.DMA((SECTIONS,)),
+            pltpu.SemaphoreType.DMA((SECTIONS, HALVES)),
+            pltpu.SemaphoreType.DMA((SECTIONS, HALVES)),
             pltpu.SemaphoreType.DMA((tile_count,)),
             pltpu.SemaphoreType.DMA((tile_count,)),
             pltpu.SemaphoreType.DMA((steps, tile_count)),
             pltpu.SemaphoreType.DMA((steps, tile_count)),
         ],
         compiler_params=pltpu.CompilerParams(
-            collective_id=0, has_side_effects=True, vmem_limit_bytes=48 * 1024 * 1024
+            collective_id=0, has_side_effects=True
         ),
         name="chain",
-    )(coarse_offsets, valid_mask, dft_hi, dft_lo, dft_t_hi, dft_t_lo, window, warp, sections)
+    )(coarse_offsets.T, valid_mask, *tables, sections)
     return pl.pallas_call(
         warp_kernel,
         out_shape=(
             jax.ShapeDtypeStruct(sections.shape, bf16),
             jax.ShapeDtypeStruct((2, 1, grid_cols), f32),
         ),
-        in_specs=[vmem, vmem, vmem],
-        out_specs=(vmem, vmem),
+        in_specs=[vmem, hbm, hbm],
+        out_specs=(hbm, vmem),
+        scratch_shapes=[
+            pltpu.VMEM((PIECES, PATCH, sections.shape[1] // PIECES), bf16),
+            pltpu.VMEM(tables[-1].shape, f32),
+            pltpu.VMEM((PIECES, PATCH, sections.shape[1] // PIECES), bf16),
+            pltpu.SemaphoreType.DMA((2 * PIECES + 1,)),
+        ],
         name="warp",
-    )(shift, sections, warp)
+    )(shift, sections, tables[-1])
 
 
 def solution(mesh):

time: 54 us -> 47.3 us (0.88)
  local copies, waits for them, and re-layouts: 7.43 us -> 0 us
  Pallas kernels: 45.4 us -> 46.5 us
    unnamed x19 -> x0, local copies, waits for them, and re-layouts: 7.43 us -> none
    pallas_call x1, Pallas kernels: 4.17 us -> 6.04 us  [shards(): pl.pallas_call(warp_kernel, out_shape=(jax.ShapeDtypeStruct(sections.shap...]
    pallas_call x1, Pallas kernels: 41.3 us -> 40.4 us  [shards(): pl.pallas_call(functools.partial(chain_kernel, tile_count, grid_cols), ou...]
where the time goes in v1:
time: 47.3 us; the launch traced here: 47.1 us
  Pallas kernels  46.5 us (98%)
  between operations  0.64 us (1%)
    pallas_call x1, Pallas kernels, shards(): pl.pallas_call(functools.partial(chain_kernel, tile_count, grid_cols), ou...  40.4 us
    pallas_call x1, Pallas kernels, shards(): pl.pallas_call(warp_kernel, out_shape=(jax.ShapeDtypeStruct(sections.shap...  6.04 us

profile of v1, /device:TPU:0, one launch (start us, length us, event | category | flops | bytes accessed | tf_op | source)
XLA Modules:
  0.0 47.1 jit_solution(12530122999722869373)
XLA Ops:
  0.6 40.4 %chain.1.shift_ref = f32[2,128]{1,0:T(2,128)} custom-call(s32[2,4]{1,0:T(2,128)} %bitcast.1, s32[1,16]{1,0:T(1,128)} %mask_in.1, bf16[256,128]{1,0:T(8,128)(2,1)} %constant.12.clone.rest_0_, bf16[256,128]{1,0:T(8,128)(2,1)} %constant.13.clone.rest_1_, bf16[128,256]{1,0:T(8,128)(2,1)} %constant.14.clone.rest_2_, bf16[128,256]{1,0:T(8,128)(2,1)} %constant.15.clone.rest_3_, ...), custom_call_target="tpu_custom_call" | custom-call | tf_op jit(solution)/shard_map/chain/pallas_call | solution.py:489
  41.0 6.0 %warp.1 = (bf16[128,2048]{1,0:T(8,128)(2,1)}, f32[2,1,16]{2,1,0:T(1,128)}) custom-call(f32[2,128]{1,0:T(2,128)} %chain.1.shift_ref, bf16[128,2048]{1,0:T(8,128)(2,1)} %strip_in.1, f32[4,128,128]{2,1,0:T(8,128)} %constant.17.clone.rest_5_.tables_in), custom_call_target="tpu_custom_call" | custom-call | tf_op jit(solution)/shard_map/warp/pallas_call | solution.py:519

commit v2 on v1

--- a/solution.py
+++ b/solution.py
@@ -18,7 +18,7 @@
 LANES = 128
 CONSTANTS = 6
 HALVES = 2
-PIECES = 4
+PIECES = 2
 
 sharpness = 12.0
 anchor_weight = 2.0
@@ -44,34 +44,30 @@
     return product(a[0], b[0]) + (product(a[0], b[1]) + product(a[1], b[0]))
 
 
-def np_split(value):
-    value = np.asarray(value, np.float32)
-    high = np.asarray(value, bf16)
-    low = np.asarray(value - high.astype(np.float32), bf16)
-    return high, low
-
-
 def constants():
     n = PATCH
     k = np.arange(n)
     angle = 2 * np.pi * ((k[:, None] * k[None, :]) % n) / n
     stacked = np.concatenate([np.cos(angle), np.sin(angle)], axis=0)
-    dft_hi, dft_lo = np_split(stacked)
-    dft_t_hi, dft_t_lo = np_split(stacked.T)
+    dft_hi = np.asarray(stacked, bf16)
+    dft_t_hi = np.asarray(stacked.T, bf16)
+    dft_lo = np.asarray(stacked - dft_hi.astype(np.float64), bf16)
+    dft_hi2 = np.concatenate([dft_hi, dft_lo], axis=0)
+    dft_t_hi2 = np.concatenate([dft_t_hi, np.asarray(stacked.T - dft_t_hi.astype(np.float64), bf16)], axis=1)
     u = np.arange(-HALF - REACH, -HALF - REACH + 24)
     window_angle = 2 * np.pi * ((u[:, None] * k[None, :]) % n) / n
-    window = np.stack([np.cos(window_angle), np.sin(window_angle)]).astype(np.float32)
-    gap = k[:, None] - k[None, :]
-    half_angle = np.pi * gap / n
-    warp = np.stack(
-        [
-            np.sin(half_angle),
-            np.cos(half_angle),
-            (1.0 - 2.0 * (gap % 2)) * np.ones((n, n)),
-            gap % n,
-        ]
-    ).astype(np.float32)
-    return dft_hi, dft_lo, dft_t_hi, dft_t_lo, window, warp
+    exact = np.cos(angle)
+    gain = (dft_hi[:n].astype(np.float64) * exact).sum(axis=1) / (exact * exact).sum(axis=1)
+    window = np.stack([np.cos(window_angle), np.sin(window_angle)])
+    window = window.astype(np.float32)
+    half_angle = np.pi * k / n
+    sign = 1.0 - 2.0 * (k % 2)
+    warp = np.zeros((8, n), np.float32)
+    warp[:4] = np.stack([np.sin(half_angle), np.cos(half_angle), sign, k])
+    parity = (sign[:, None] * sign[None, :]).astype(np.float32)
+    sums = (dft_hi.astype(np.float64)+dft_lo.astype(np.float64)).sum(axis=1, keepdims=True)
+    sums = np.broadcast_to(sums, (2 * n, n)).astype(np.float32)
+    return dft_hi2, dft_t_hi2, sums, window, warp, parity
 
 
 def shift_terms(d):
@@ -90,29 +86,40 @@
     return tangent, signed, peak, whole
 
 
-def interpolation(terms, tables, transposed):
-    tangent, signed, peak, whole = terms
-    sine, cosine, parity, gap = tables
-    if transposed:
-        bottom = cosine * tangent - sine
-        top = cosine + sine * tangent
-        centre = jnp.where(whole < 0, whole + PATCH, whole)
-    else:
-        bottom = cosine * tangent + sine
-        top = cosine - sine * tangent
-        centre = jnp.where(whole > 0, PATCH - whole, -whole)
-    value = jnp.where(gap == centre, peak, (signed * parity) * (top / bottom))
-    return split(value)
-
-
-def warp_patch(patch, column, checker, tables):
-    row_terms = [column[i : i + 1, :] for i in range(4)]
-    col_terms = [column[i : i + 1, :] for i in range(4, 8)]
-    right = interpolation(col_terms, tables, True)
-    left = interpolation(row_terms, tables, False)
-    inner = split(mm(patch, right[0]) + mm(patch, right[1]))
-    corner = row_terms[1] * col_terms[1] * checker
-    return mm3(left, inner) - corner * tables[2]
+def kernel_rows(terms, tables):
+    columns = jnp.transpose(terms)[:LANES]
+    sine, cosine, parity, gap = [tables[i : i + 1, :] for i in range(4)]
+    found = []
+    for base, forward in ((0, False), (4, True)):
+        tangent, signed, peak, whole = [columns[:, base + i : base + i + 1] for i in range(4)]
+        if forward:
+            bottom = cosine * tangent + sine
+            top = cosine - sine * tangent
+            centre = jnp.where(whole > 0, PATCH - whole, -whole)
+        else:
+            bottom = cosine * tangent - sine
+            top = cosine + sine * tangent
+            centre = jnp.where(whole < 0, whole + PATCH, whole)
+        found.append(jnp.where(gap == centre, peak, (signed * parity) * (top / bottom)))
+    corner = columns[:, 1:2] * columns[:, 5:6]
+    return found[0], found[1], corner
+
+
+def circulant(row):
+    spread = jnp.broadcast_to(row, (PATCH, PATCH))
+    return split(pltpu.roll(spread, 0, 1, stride=1, stride_axis=0))
+
+
+def warp_patch(patch, rows, i, checker, parity):
+    left = circulant(rows[0][i : i + 1, :])
+    right = circulant(rows[1][i : i + 1, :])
+    both = mm(patch, jnp.concatenate(right, axis=1))
+    high, low = split(both[:, :PATCH] + both[:, PATCH:])
+    lower = jnp.concatenate([high, jnp.zeros_like(low)], axis=1)
+    inner = jnp.concatenate([jnp.concatenate([high, low], axis=1), lower], axis=0)
+    moved = mm(jnp.concatenate(left, axis=1), inner)
+    corner = (rows[2][i : i + 1, :] * checker) * parity
+    return (moved[:, :PATCH] + moved[:, PATCH:]) - corner
 
 
 def total(value):
@@ -130,7 +137,7 @@
     mean_level = total(patch) * (1.0 / (PATCH * PATCH))
     centre = patch - mean_level
     variance = total(centre * centre) * (1.0 / (PATCH * PATCH))
-    return centre, jnp.sqrt(variance + 1e-05)
+    return mean_level, jnp.sqrt(variance + 1e-05)
 
 
 def patch_slices(width):
@@ -146,7 +153,7 @@
 ):
     constant_in = rest[:CONSTANTS]
     constant_ref = rest[CONSTANTS + 2 : 2 * CONSTANTS + 2]
-    (dft_hi, dft_lo, dft_t_hi, dft_t_lo, window, warp_tables) = constant_ref
+    dft_ref, dft_t_ref, sums_ref, window, warp_tables, parity_ref = constant_ref
     strip, out_ref = rest[CONSTANTS : CONSTANTS + 2]
     (
     offsets,
@@ -242,16 +249,19 @@
             sends.append(copy)
     for copy in loads[1:]:
         copy.wait()
-    tables = [warp_tables[i] for i in range(4)]
-    dft = (dft_hi[...], dft_lo[...])
-    dft_t = (dft_t_hi[...], dft_t_lo[...])
-
-    def spectra(centres):
-        strip0 = jnp.concatenate(centres, axis=1)
-        first = split(mm3(dft, split(strip0)))
+    tables = warp_tables[...]
+    parity = parity_ref[...]
+    dft = dft_ref[...]
+    dft_t = dft_t_ref[...]
+    sums = sums_ref[...]
+
+    def spectra(patches, levels):
         found = []
-        for s in patch_slices(strip0.shape[1]):
-            both = mm3((first[0][:, s], first[1][:, s]), dft_t)
+        for patch, level in zip(patches, levels):
+            first = mm(dft, patch)
+            first = (first[: 2 * PATCH] + first[2 * PATCH :] - sums * level).astype(bf16)
+            both = mm(first, dft_t)
+            both = both[:, : 2 * PATCH] + both[:, 2 * PATCH :]
             real = both[:PATCH, :PATCH] - both[PATCH:, PATCH:]
             imag = -(both[:PATCH, PATCH:] + both[PATCH:, :PATCH])
             found.append((real, imag))
@@ -262,15 +272,16 @@
         return raw[section, i // part_nodes, :, start : start + PATCH]
 
     def own_spectra(section, nodes):
-        pieces = [centred(patch_of(section, i).astype(f32)) for i in nodes]
-        found = spectra([piece[0] for piece in pieces])
+        patches = [patch_of(section, i) for i in nodes]
+        pieces = [centred(patch.astype(f32)) for patch in patches]
+        found = spectra(patches, [piece[0] for piece in pieces])
         for i, (real, imag) in zip(nodes, found):
             spec_re[i] = real
             spec_im[i] = imag
         return [piece[1] for piece in pieces]
 
     def checkers(section):
-        return [total(patch_of(section, i).astype(f32) * tables[2]) for i in range(quarter_nodes)]
+        return [total(patch_of(section, i).astype(f32) * parity) for i in range(quarter_nodes)]
 
     up_ok = (sub_row > 0).astype(f32)
     down_ok = (sub_row < per_section - 1).astype(f32)
@@ -303,15 +314,15 @@
         ).wait()
 
     def flows(section, previous, own_spread, nodes):
-        pieces = [centred(patch) for patch in previous]
-        found = spectra([piece[0] for piece in pieces])
+        pieces = [centred(patch.astype(f32)) for patch in previous]
+        found = spectra(previous, [piece[0] for piece in pieces])
         row_offset = offsets[0, section]
         col_offset = offsets[1, section]
         row_cos = window[0, pl.ds(row_offset + REACH, PADDED), :]
         row_sin = window[1, pl.ds(row_offset + REACH, PADDED), :]
         col_cos = split(window[0, pl.ds(col_offset + REACH, PADDED), :])
         col_sin = split(window[1, pl.ds(col_offset + REACH, PADDED), :])
-        row_table = split(jnp.concatenate([row_cos, row_sin], axis=0))
+        row_table = jnp.concatenate(split(jnp.concatenate([row_cos, row_sin], axis=0)), axis=0)
         row_shift = (corr_row - HALF + row_offset).astype(f32)
         col_shift = (corr_col - HALF + col_offset).astype(f32)
         half_re, half_im = [], []
@@ -319,8 +330,11 @@
             own_re, own_im = spec_re[i], spec_im[i]
             cross_re = own_re * prev_re + own_im * prev_im
             cross_im = own_im * prev_re - own_re * prev_im
-            part_re = mm3(row_table, split(cross_re))
-            part_im = mm3(row_table, split(cross_im))
+            cross = jnp.concatenate([cross_re, cross_im], axis=1).astype(bf16)
+            parts = mm(row_table, cross)
+            parts = parts[: 2 * PADDED] + parts[2 * PADDED :]
+            part_re = parts[:, :PATCH]
+            part_im = parts[:, PATCH:]
             half_re.append(part_re[:PADDED] - part_im[PADDED:])
             half_im.append(part_im[:PADDED] + part_re[PADDED:])
         correlation = mm3(
@@ -375,7 +389,7 @@
                 arrived(1, half)
                 arrived(0, half)
                 spread = own_spectra(1, nodes)
-                previous = [patch_of(0, i).astype(f32) for i in nodes]
+                previous = [patch_of(0, i) for i in nodes]
                 tile = tile + flows(1, previous, spread, nodes)
         else:
             pick_rows = jnp.sum(
@@ -386,12 +400,16 @@
             )
             terms = term_rows(pick_rows, pick_cols)
             term_lane = lax.broadcasted_iota(jnp.int32, terms.shape, 1)
-            previous = []
+            placed = jnp.zeros(terms.shape, f32)
             for i in everyone:
                 wanted = term_lane == chain * quarter_nodes + i
                 column = jnp.sum(jnp.where(wanted, terms, 0.0), axis=1, keepdims=True)
-                moved = warp_patch(patch_of(index, i), column, corners[i], tables)
-                previous.append(moved.astype(bf16).astype(f32))
+                placed = jnp.where(term_lane == i, column, placed)
+            rows = kernel_rows(placed, tables)
+            previous = [
+                warp_patch(patch_of(index, i), rows, i, corners[i], parity).astype(bf16)
+                for i in everyone
+            ]
             tile = flows(section, previous, spread, everyone)
         flow_tile[index] = tile
         flow_sum[index] = tile
@@ -443,11 +461,11 @@
     out_ref[...] = jnp.concatenate([out_row, out_col], axis=0)
 
 
-def warp_kernel(shift_ref, strip_in, tables_in, out, node_ref, strip, warp_tables, result, sems):
+def warp_kernel(
+    shift_ref, strip_in, warp_tables, parity_ref, out, node_ref, strip, result, sems
+):
     pieces = strip.shape[0]
     width = strip.shape[2]
-    table_load = pltpu.make_async_copy(tables_in, warp_tables, sems.at[2 * pieces])
-    table_load.start()
     loads, stores = [], []
     for k in range(pieces):
         where = pl.ds(k * width, width)
@@ -456,21 +474,18 @@
             pltpu.make_async_copy(result.at[k], out.at[:, where], sems.at[pieces + k])
         )
         loads[k].start()
-    terms = term_rows(shift_ref[0:1, :], shift_ref[1:2, :])
-    lane = lax.broadcasted_iota(jnp.int32, terms.shape, 1)
     nodes = node_ref.shape[2]
     node_ref[0] = shift_ref[0:1, 0:nodes]
     node_ref[1] = shift_ref[1:2, 0:nodes]
-    table_load.wait()
-    tables = [warp_tables[i] for i in range(4)]
+    rows = kernel_rows(term_rows(shift_ref[0:1, :], shift_ref[1:2, :]), warp_tables[...])
+    parity = parity_ref[...]
     for k in range(pieces):
         loads[k].wait()
         for j, s in enumerate(patch_slices(width)):
             i = k * (width // PATCH) + j
-            column = jnp.sum(jnp.where(lane == i, terms, 0.0), axis=1, keepdims=True)
             patch = strip[k, :, s]
-            checker = total(patch.astype(f32) * tables[2])
-            result[k, :, s] = warp_patch(patch, column, checker, tables).astype(bf16)
+            checker = total(patch.astype(f32) * parity)
+            result[k, :, s] = warp_patch(patch, rows, i, checker, parity).astype(bf16)
         stores[k].start()
     for copy in stores:
         copy.wait()
@@ -522,16 +537,15 @@
             jax.ShapeDtypeStruct(sections.shape, bf16),
             jax.ShapeDtypeStruct((2, 1, grid_cols), f32),
         ),
-        in_specs=[vmem, hbm, hbm],
+        in_specs=[vmem, hbm, vmem, vmem],
         out_specs=(hbm, vmem),
         scratch_shapes=[
             pltpu.VMEM((PIECES, PATCH, sections.shape[1] // PIECES), bf16),
-            pltpu.VMEM(tables[-1].shape, f32),
             pltpu.VMEM((PIECES, PATCH, sections.shape[1] // PIECES), bf16),
-            pltpu.SemaphoreType.DMA((2 * PIECES + 1,)),
+            pltpu.SemaphoreType.DMA((2 * PIECES,)),
         ],
         name="warp",
-    )(shift, sections, tables[-1])
+    )(shift, sections, tables[-2], tables[-1])
 
 
 def solution(mesh):

time: 47.3 us -> 45.2 us (0.956)
  Pallas kernels: 46.5 us -> 44.3 us
    pallas_call x1, Pallas kernels: 6.04 us -> 4.49 us  [shards(): pl.pallas_call(warp_kernel, out_shape=(jax.ShapeDtypeStruct(sections.shap...]
    pallas_call x1, Pallas kernels: 40.4 us -> 39.9 us  [shards(): pl.pallas_call(functools.partial(chain_kernel, tile_count, grid_cols), ou...]
where the time goes in v2:
time: 45.2 us; the launch traced here: 45 us
  Pallas kernels  44.3 us (98%)
  between operations  0.64 us (1%)
    pallas_call x1, Pallas kernels, shards(): pl.pallas_call(functools.partial(chain_kernel, tile_count, grid_cols), ou...  39.9 us
    pallas_call x1, Pallas kernels, shards(): pl.pallas_call(warp_kernel, out_shape=(jax.ShapeDtypeStruct(sections.shap...  4.49 us

profile of v2, /device:TPU:0, one launch (start us, length us, event | category | flops | bytes accessed | tf_op | source)
XLA Modules:
  0.0 45.0 jit_solution(9505668731884425519)
XLA Ops:
  0.6 39.9 %chain.1.shift_ref = f32[2,128]{1,0:T(2,128)} custom-call(s32[2,4]{1,0:T(2,128)} %bitcast.1, s32[1,16]{1,0:T(1,128)} %mask_in.1, bf16[512,128]{1,0:T(8,128)(2,1)} %constant.12.clone.rest_0_, bf16[128,512]{1,0:T(8,128)(2,1)} %constant.13.clone.rest_1_, f32[256,128]{1,0:T(8,128)} %constant.14.clone.rest_2_, f32[2,24,128]{2,1,0:T(8,128)} %constant.15.clone.rest_3_, ...), custom_call_target="tpu_custom_call" | custom-call | tf_op jit(solution)/shard_map/chain/pallas_call | solution.py:504
  40.5 4.5 %warp.1 = (bf16[128,2048]{1,0:T(8,128)(2,1)}, f32[2,1,16]{2,1,0:T(1,128)}) custom-call(f32[2,128]{1,0:T(2,128)} %chain.1.shift_ref, bf16[128,2048]{1,0:T(8,128)(2,1)} %strip_in.1, f32[8,128]{1,0:T(8,128)} %constant.16.clone.rest_4_.warp_tables, f32[128,128]{1,0:T(8,128)} %constant.17.clone.rest_5_.parity_ref), custom_call_target="tpu_custom_call" | custom-call | tf_op jit(solution)/shard_map/warp/pallas_call | solution.py:534
